TPU v7x, 32 devices: a whole 2x2x4 slice. The times are simulated.
32 devices in a mesh: dp: 2 (over x), row: 4 (over z), col: 4 (over y, core).
Axes of the slice: x: 2, y: 2, z: 4, core: 2. Of those that a mesh axis runs over, the one named last changes fastest.
Arguments:
- tokens: bfloat16 [4, 2048, 2048], P('dp', 'row', 'col'), may hold values from -6 to 6
- lengths: int32 [4], P('dp'), may hold values from 682 to 2048, as said below
- cotangent: bfloat16 [4, 2048, 2048], P('dp', 'row', 'col'), may hold values from -6 to 6
- norm1_gain: float32 [2048], P('col'), may hold values from 0.25 to 1.75
- norm1_bias: float32 [2048], P('col'), may hold values from -3 to 3
- query_weight: bfloat16 [2048, 2048], P('col', 'row'), may hold values from -0.125 to 0.125
- kv_weight: bfloat16 [2048, 256], P('col'), may hold values from -0.125 to 0.125
- out_weight: bfloat16 [2048, 2048], P('row', 'col'), may hold values from -1 to 1
- norm2_gain: float32 [2048], P('col'), may hold values from 0.25 to 1.75
- norm2_bias: float32 [2048], P('col'), may hold values from -3 to 3
- up_weight: bfloat16 [2048, 8192], P('col', 'row'), may hold values from -0.125 to 0.125
- down_weight: bfloat16 [8192, 2048], P('row', 'col'), may hold values from -0.0625 to 0.0625
Outputs:
- out: bfloat16 [4, 2048, 2048], P('dp', 'row', 'col')
- grad_input: bfloat16 [4, 2048, 2048], P('dp', 'row', 'col')
- grad_norm1_gain: float32 [2048], P('col')
- grad_norm1_bias: float32 [2048], P('col')
- grad_query_weight: float32 [2048, 2048], P('col', 'row')
- grad_kv_weight: float32 [2048, 256], P('col')
- grad_out_weight: float32 [2048, 2048], P('row', 'col')
- grad_norm2_gain: float32 [2048], P('col')
- grad_norm2_bias: float32 [2048], P('col')
- grad_up_weight: float32 [2048, 8192], P('col', 'row')
- grad_down_weight: float32 [8192, 2048], P('row', 'col')
Inputs may be any that keep to these rules, and one draw needn't show every extreme that they name: `lengths`: entry s is the number of valid slots of sequence s; sequences s * 2 to s * 2 + 1 belong to index s of dp. Some sequence has all 2048 slots valid.
All inputs are finite; a program needn't handle non-finite values.
Results may differ from a plain program's by a relative error of at most 0.02.
Values may be sent and summed in bfloat16 or wider, within the bound.
A program may use at most 256 MiB of HBM per device.

v0:
```python
import jax
import jax.numpy as jnp
from jax import lax
from jax.sharding import PartitionSpec as P

eps = 1e-05
BF = jnp.bfloat16
F32 = jnp.float32


def mm(a, b, ca, cb):
    return lax.dot_general(a, b, (((ca,), (cb,)), ((), ())), preferred_element_type=F32)


def norm_stats(hidden):
    centre = jnp.mean(hidden, axis=1, keepdims=True)
    spread = jnp.mean(hidden * hidden, axis=1, keepdims=True) - centre * centre
    return (centre, lax.rsqrt(spread + eps))


def norm_apply(hidden, centre, inverse, gain, bias, keep):
    return (keep * ((hidden - centre) * inverse * gain + bias)).astype(BF)


def norm_backward(gradient, normed, inverse, gain, keep):
    masked = keep * gradient
    scaled = masked * gain
    first = jnp.mean(scaled, axis=1, keepdims=True)
    second = jnp.mean(scaled * normed, axis=1, keepdims=True)
    result = inverse * (scaled - first - normed * second)
    return (result, jnp.sum(masked * normed, axis=0), jnp.sum(masked, axis=0))


def turn(weight):
    return lax.all_to_all(weight, "col", 0, 1, tiled=True)


def turn_back(rows):
    return lax.all_to_all(rows, "col", 1, 0, tiled=True)


def gather(x, axes, dim=0):
    return lax.all_gather(x, axes, axis=dim, tiled=True)


def scatter(x, axes):
    return lax.psum_scatter(x, axes, scatter_dimension=0, tiled=True)


def pairs_allowed(first, count, keys, length):
    q = first + jnp.arange(count, dtype=jnp.int32)[:, None]
    k = jnp.arange(keys, dtype=jnp.int32)[None, :]
    return (k <= q) & (k < length)


def attend(queries, kv, lengths, first):
    b, t, width = queries.shape
    hd = kv.shape[2] // 2
    outs, logs = ([], [])
    for s in range(b):
        keys, values = (kv[s, :, :hd], kv[s, :, hd:])
        allowed = pairs_allowed(first, t, kv.shape[1], lengths[s])
        for h in range(width // hd):
            q = queries[s, :, h * hd : (h + 1) * hd]
            scores = jnp.where(allowed, mm(q, keys, 1, 1) * hd ** (-0.5), -jnp.inf)
            top = jnp.max(scores, axis=1, keepdims=True)
            log_total = top + jnp.log(jnp.sum(jnp.exp(scores - top), axis=1, keepdims=True))
            weights = jnp.exp(scores - log_total).astype(BF)
            outs.append(mm(weights, values, 1, 0).astype(BF))
            logs.append(log_total)
    n = width // hd
    out = jnp.stack([jnp.concatenate(outs[s * n : (s + 1) * n], axis=1) for s in range(b)])
    log = jnp.stack([jnp.concatenate(logs[s * n : (s + 1) * n], axis=1) for s in range(b)])
    return (out, log)


def attend_back(queries, kv, lengths, first, logs, grad):
    b, t, width = queries.shape
    hd = kv.shape[2] // 2
    scale = hd ** (-0.5)
    dqs, dkvs = ([], [])
    for s in range(b):
        keys, values = (kv[s, :, :hd], kv[s, :, hd:])
        allowed = pairs_allowed(first, t, kv.shape[1], lengths[s])
        dk = dv = 0.0
        dq = []
        for h in range(width // hd):
            q = queries[s, :, h * hd : (h + 1) * hd]
            g = grad[s, :, h * hd : (h + 1) * hd]
            scores = jnp.where(allowed, mm(q, keys, 1, 1) * scale, -jnp.inf)
            p = jnp.exp(scores - logs[s, :, h : h + 1])
            dp = mm(g, values, 1, 1)
            ds = (p * (dp - jnp.sum(p * dp, axis=1, keepdims=True))).astype(BF)
            dq.append((mm(ds, keys, 1, 0) * scale).astype(BF))
            dk = dk + mm(ds, q, 0, 0) * scale
            dv = dv + mm(p.astype(BF), g, 0, 0)
        dqs.append(jnp.concatenate(dq, axis=1))
        dkvs.append(jnp.concatenate([dk, dv], axis=1).astype(BF))
    return (jnp.stack(dqs), jnp.stack(dkvs))


def local(
    tokens,
    lengths,
    cotangent,
    norm1_gain,
    norm1_bias,
    query_weight,
    kv_weight,
    out_weight,
    norm2_gain,
    norm2_bias,
    up_weight,
    down_weight,
):
    b, t, f = tokens.shape
    nd, nr, nc = (lax.axis_size(a) for a in ("dp", "row", "col"))
    dp, row, col = (lax.axis_index(a) for a in ("dp", "row", "col"))
    m, d = (b * t, f * nc)
    own = m // nc
    hd = kv_weight.shape[1] // 2
    plane = ("dp", "col")
    slot = row * t + jnp.arange(t, dtype=jnp.int32)
    keep = (slot[None, :] < lengths[:, None]).astype(F32).reshape(m, 1)

    def mine(x):
        return lax.dynamic_slice_in_dim(x, col * own, own, 0)

    def half(w):
        n = w.shape[0] // nd
        return lax.dynamic_slice_in_dim(w, dp * n, n, 0)

    wq = gather(turn(query_weight.T), "row")
    wo = gather(turn(out_weight), "row")
    wu = gather(turn(half(up_weight.T)), "row")
    wd = gather(turn(half(down_weight)), "row")
    wkv = gather(kv_weight, "col")
    vectors = gather(jnp.stack([norm1_gain, norm1_bias, norm2_gain, norm2_bias]), "col", 1)
    gain1, bias1, gain2, bias2 = (vectors[i : i + 1] for i in range(4))
    x = gather(tokens.reshape(m, f), "col", 1)
    grad_final = (keep * cotangent.reshape(m, f).astype(F32)).astype(BF)
    grad_own = turn(grad_final)
    grad_all = gather(grad_own, plane)
    keep_own = mine(keep)
    centre, inverse = norm_stats(x.astype(F32))
    one = norm_apply(x.astype(F32), centre, inverse, gain1, bias1, keep)
    one_own = mine(one)
    queries = mm(one, wq, 1, 1).astype(BF).reshape(b, t, -1)
    kv_own = mm(one_own, wkv, 1, 0).astype(BF)
    kv = gather(kv_own, ("row", "col")).reshape(nr, b, t, 2 * hd)
    kv = kv.transpose(1, 0, 2, 3).reshape(b, nr * t, 2 * hd)
    attended, logs = attend(queries, kv, lengths, row * t)
    attended = attended.reshape(m, -1)
    x_own = mine(x).astype(F32)
    middle = x_own + scatter(mm(attended, wo, 1, 0).astype(BF), "col").astype(F32)
    centre2, inverse2 = norm_stats(middle)
    two_own = norm_apply(middle, centre2, inverse2, gain2, bias2, keep_own)
    two = gather(two_own, plane)
    sums = mm(two, wu, 1, 1)
    activated, pull = jax.vjp(lambda v: jax.nn.gelu(v, approximate=True), sums)
    activated = activated.astype(BF)
    ffn = scatter(mm(activated, wd, 1, 0).astype(BF), plane)
    out = turn_back((keep_own * (middle + ffn.astype(F32))).astype(BF))
    grad_act = mm(grad_all, wd, 1, 1)
    grad_up = pull(grad_act)[0].astype(BF)
    d_down = scatter(mm(activated, grad_all, 0, 0).astype(BF), "row")
    d_up = scatter(mm(grad_up, two, 0, 0).astype(BF), "row")
    e_two = scatter(mm(grad_up, wu, 1, 0).astype(BF), plane).astype(F32)
    normed2 = (middle - centre2) * inverse2
    back_two, g_gain2, g_bias2 = norm_backward(e_two, normed2, inverse2, gain2, keep_own)
    grad_middle = grad_own.astype(F32) + back_two
    grad_attn = gather(grad_middle.astype(BF), "col")
    grad_att = mm(grad_attn, wo, 1, 1).astype(BF)
    d_out = scatter(mm(attended, grad_attn, 0, 0).astype(BF), "row")
    dq, dkv = attend_back(queries, kv, lengths, row * t, logs, grad_att.reshape(b, t, -1))
    dq = dq.reshape(m, -1)
    dkv = dkv.reshape(b, nr, t, 2 * hd).transpose(1, 0, 2, 3).reshape(nr * m, 2 * hd)
    dkv_own = scatter(dkv, ("row", "col"))
    d_query = scatter(mm(dq, one, 0, 0).astype(BF), "row")
    e_one = scatter(mm(dq, wq, 1, 0).astype(BF), "col").astype(F32) + mm(dkv_own, wkv, 1, 1)
    normed1 = (x_own - mine(centre)) * mine(inverse)
    back_one, g_gain1, g_bias1 = norm_backward(e_one, normed1, mine(inverse), gain1, keep_own)
    grad_in = turn_back((grad_middle + back_one).astype(BF))
    d_kv = scatter(mm(one_own, dkv_own, 0, 0).astype(BF), "col")
    d_kv = lax.psum(d_kv, ("dp", "row")).astype(F32)
    small = lax.psum(jnp.stack([g_gain1, g_bias1, g_gain2, g_bias2]), ("dp", "row", "col"))
    small = lax.dynamic_slice_in_dim(small, col * f, f, 1)
    d_query = lax.psum(turn_back(d_query), "dp").astype(F32).T
    d_out = lax.psum(turn_back(d_out), "dp").astype(F32)
    d_up = gather(turn_back(d_up), "dp").astype(F32).T
    d_down = gather(turn_back(d_down), "dp").astype(F32)
    return (
        out.reshape(b, t, f),
        grad_in.reshape(b, t, f),
        small[0],
        small[1],
        d_query,
        d_kv,
        d_out,
        small[2],
        small[3],
        d_up,
        d_down,
    )


def solution(mesh):
    act, vec = (P("dp", "row", "col"), P("col"))
    wide, tall = (P("col", "row"), P("row", "col"))
    return jax.shard_map(
        local,
        mesh=mesh,
        in_specs=(act, P("dp"), act, vec, vec, wide, P("col", None), tall, vec, vec, wide, tall),
        out_specs=(act, act, vec, vec, wide, P("col", None), tall, vec, vec, wide, tall),
        check_vma=False,
    )
```

profile of v0, /device:TPU:0, one launch (start us, length us, event | category | flops | bytes accessed | tf_op | source)
XLA Modules:
  0.0 1477.3 jit_solution(9713727474657189356)
XLA Ops:
  82.3 31.9 %all-gather.15.cloned.1.call-done = bf16[512,2048]{0,1:T(8,128)(2,1)} async-done(((bf16[128,2048]{0,1:T(8,128)(2,1)}), bf16[512,2048]{0,1:T(8,128)(2,1)}) %all-gather.15.cloned.1.call-update) | async-done | bytes 2097168 | tf_op jit(solution)/shard_map/all_gather | solution.py:43
  119.4 37.1 %all-gather.19.cloned.1.call-done = bf16[4096,256]{1,0:T(8,128)(2,1)} async-done(((bf16[256,256]{1,0:T(8,128)(2,1)}), bf16[4096,256]{1,0:T(8,128)(2,1)}) %all-gather.19.cloned.1.call-update) | async-done | bytes 2097168 | tf_op jit(solution)/shard_map/all_gather | solution.py:43
  184.7 18.8 %all-gather.21.cloned.1.call-done = bf16[512,2048]{0,1:T(8,128)(2,1)} async-done(((bf16[128,2048]{0,1:T(8,128)(2,1)}), bf16[512,2048]{0,1:T(8,128)(2,1)}) %all-gather.21.cloned.1.call-update) | async-done | bytes 2097168 | tf_op jit(solution)/shard_map/all_gather | solution.py:43
  229.1 28.4 %all_to_all.202 = bf16[4,256,512]{2,1,0:T(8,128)(2,1)S(1)} all-to-all(bf16[4,256,512]{2,1,0:T(8,128)(2,1)S(1)} %fusion.58), channel_id=1, replica_groups=mesh['dp'=2,'row'=4,'col'=4] {'col'}, dimensions={0} | all-to-all | bytes 2097152 | tf_op jit(solution)/shard_map/all_to_all | solution.py:35
  284.8 62.0 %all-gather.27.cloned.1.call-done = bf16[1024,2048]{0,1:T(8,128)(2,1)} async-done(((bf16[256,2048]{0,1:T(8,128)(2,1)}), bf16[1024,2048]{0,1:T(8,128)(2,1)}) %all-gather.27.cloned.1.call-update) | async-done | bytes 4194320 | tf_op jit(solution)/shard_map/all_gather | solution.py:43
  346.8 55.2 %all-gather.29.cloned.1.call-done = bf16[2048,2048]{1,0:T(8,128)(2,1)} async-done(((bf16[256,2048]{1,0:T(8,128)(2,1)}), bf16[2048,2048]{1,0:T(8,128)(2,1)}) %all-gather.29.cloned.1.call-update) | async-done | bytes 8388624 | tf_op jit(solution)/shard_map/all_gather | solution.py:43
  416.4 67.8 %all-gather.25.cloned.1.call-done = bf16[1024,2048]{0,1:T(8,128)(2,1)} async-done(((bf16[256,2048]{0,1:T(8,128)(2,1)}), bf16[1024,2048]{0,1:T(8,128)(2,1)}) %all-gather.25.cloned.1.call-update) | async-done | bytes 4194320 | tf_op jit(solution)/shard_map/all_gather | solution.py:43
  484.2 55.1 %all-gather.23.cloned.1.call-done = bf16[2048,2048]{1,0:T(8,128)(2,1)} async-done(((bf16[256,2048]{1,0:T(8,128)(2,1)}), bf16[2048,2048]{1,0:T(8,128)(2,1)}) %all-gather.23.cloned.1.call-update) | async-done | bytes 8388624 | tf_op jit(solution)/shard_map/all_gather | solution.py:43
  539.3 22.2 %fusion.6 = (bf16[2048,1024]{1,0:T(8,128)(2,1)S(1)}, f32[2048,1024]{1,0:T(8,128)}) fusion(f32[2048,1024]{1,0:T(8,128)} %fusion.125, bf16[2048,2048]{1,0:T(8,128)(2,1)} %all-gather.23.cloned.1.call-done, bf16[1024,2048]{0,1:T(8,128)(2,1)} %all-gather.25.cloned.1.call-done), kind=kOutput, calls=%fused_computation.11 | convolution fusion | flops 8631877632 | bytes 33554432 | tf_op jit(solution)/shard_map/dot_general | solution.py:12
  590.0 55.9 %reduce-scatter.15.cloned.1.call-done = bf16[256,2048]{1,0:T(8,128)(2,1)} async-done(((bf16[2048,2048]{1,0:T(8,128)(2,1)}), bf16[256,2048]{1,0:T(8,128)(2,1)}) %reduce-scatter.15.cloned.1.call-update) | async-done | bytes 1048592 | tf_op jit(solution)/shard_map/reduce_scatter | solution.py:47
  648.7 71.8 %reduce-scatter.13.cloned.1.call-done = bf16[256,2048]{1,0:T(8,128)(2,1)} async-done(((bf16[2048,2048]{1,0:T(8,128)(2,1)}), bf16[256,2048]{1,0:T(8,128)(2,1)}) %reduce-scatter.13.cloned.1.call-update) | async-done | bytes 1048592 | tf_op jit(solution)/shard_map/reduce_scatter | solution.py:47
  725.9 34.5 %all-gather.31.cloned.1.call-done = bf16[1024,2048]{1,0:T(8,128)(2,1)} async-done(((bf16[256,2048]{1,0:T(8,128)(2,1)}), bf16[1024,2048]{1,0:T(8,128)(2,1)}) %all-gather.31.cloned.1.call-update) | async-done | bytes 4194320 | tf_op jit(solution)/shard_map/all_gather | solution.py:43
  913.4 75.8 %reduce-scatter.29.cloned.1.call-done = bf16[256,2048]{1,0:T(8,128)(2,1)} async-done(((bf16[1024,2048]{1,0:T(8,128)(2,1)}), bf16[256,2048]{1,0:T(8,128)(2,1)}) %reduce-scatter.29.cloned.1.call-update) | async-done | bytes 1048592 | tf_op jit(solution)/shard_map/reduce_scatter | solution.py:47
  990.5 17.6 %all_to_all.204 = bf16[256,4,512]{2,0,1:T(8,128)(2,1)} all-to-all(bf16[256,4,512]{2,0,1:T(8,128)(2,1)S(1)} %bitcast.415), channel_id=1, replica_groups=mesh['dp'=2,'row'=4,'col'=4] {'col'}, dimensions={1} | all-to-all | bytes 2097152 | tf_op jit(solution)/shard_map/all_to_all | solution.py:39
  1014.3 54.5 %reduce-scatter.27.cloned.1.call-done = bf16[256,2048]{1,0:T(8,128)(2,1)} async-done(((bf16[1024,2048]{1,0:T(8,128)(2,1)}), bf16[256,2048]{1,0:T(8,128)(2,1)}) %reduce-scatter.27.cloned.1.call-update) | async-done | bytes 1048592 | tf_op jit(solution)/shard_map/reduce_scatter | solution.py:47
  1088.5 26.9 %reduce-scatter.21.cloned.1.call-done = bf16[128,2048]{1,0:T(8,128)(2,1)} async-done(((bf16[512,2048]{1,0:T(8,128)(2,1)}), bf16[128,2048]{1,0:T(8,128)(2,1)}) %reduce-scatter.21.cloned.1.call-update) | async-done | bytes 524304 | tf_op jit(solution)/shard_map/reduce_scatter | solution.py:47
  1120.7 40.1 %reduce-scatter.25.cloned.1.call-done = bf16[128,2048]{1,0:T(8,128)(2,1)} async-done(((bf16[512,2048]{1,0:T(8,128)(2,1)}), bf16[128,2048]{1,0:T(8,128)(2,1)}) %reduce-scatter.25.cloned.1.call-update) | async-done | bytes 524304 | tf_op jit(solution)/shard_map/reduce_scatter | solution.py:47
  1166.3 21.8 %reduce-scatter.23.cloned.1.call-done = bf16[512,256]{1,0:T(8,128)(2,1)} async-done(((bf16[2048,256]{1,0:T(8,128)(2,1)}), bf16[512,256]{1,0:T(8,128)(2,1)}) %reduce-scatter.23.cloned.1.call-update) | async-done | bytes 262160 | tf_op jit(solution)/shard_map/reduce_scatter | solution.py:47
  1189.6 33.1 %all-gather.35.cloned.1.call-done = bf16[2048,512]{1,0:T(8,128)(2,1)} async-done(((bf16[1024,512]{1,0:T(8,128)(2,1)}), bf16[2048,512]{1,0:T(8,128)(2,1)}) %all-gather.35.cloned.1.call-update) | async-done | bytes 2097168 | tf_op jit(solution)/shard_map/all_gather | solution.py:43
  1233.2 37.7 %reduce-scatter.17.cloned.1.call-done = bf16[256,2048]{1,0:T(8,128)(2,1)} async-done(((bf16[1024,2048]{1,0:T(8,128)(2,1)}), bf16[256,2048]{1,0:T(8,128)(2,1)}) %reduce-scatter.17.cloned.1.call-update) | async-done | bytes 1048592 | tf_op jit(solution)/shard_map/reduce_scatter | solution.py:47
  1281.4 24.4 %all-gather.33.cloned.1.call-done = bf16[2048,512]{0,1:T(8,128)(2,1)} async-done(((bf16[1024,512]{0,1:T(8,128)(2,1)}), bf16[2048,512]{0,1:T(8,128)(2,1)}) %all-gather.33.cloned.1.call-update) | async-done | bytes 2097168 | tf_op jit(solution)/shard_map/all_gather | solution.py:43
  1310.1 69.8 %all-reduce.4.cloned.1.call-done = bf16[512,256]{1,0:T(8,128)(2,1)} async-done(((bf16[512,256]{1,0:T(8,128)(2,1)}), bf16[512,256]{1,0:T(8,128)(2,1)}) %all-reduce.4.cloned.1.call-update) | async-done | bytes 262160 | tf_op jit(solution)/shard_map/psum | solution.py:185
  1381.6 40.7 %all-reduce.6.cloned.1.call-done = (bf16[512,512]{1,0:T(8,128)(2,1)}, bf16[512,512]{1,0:T(8,128)(2,1)}) async-done(((bf16[512,512]{1,0:T(8,128)(2,1)}, bf16[512,512]{1,0:T(8,128)(2,1)}), (bf16[512,512]{1,0:T(8,128)(2,1)}, bf16[512,512]{1,0:T(8,128)(2,1)})) %all-reduce.6.cloned.1.call-update) | async-done | bytes 1048592 | tf_op jit(solution)/shard_map/psum | solution.py:188
  1426.6 39.5 %psum.28 = f32[4,2048]{1,0:T(4,128)S(1)} all-reduce(f32[4,2048]{1,0:T(4,128)S(1)} %pad_maximum_fusion.2), channel_id=1, replica_groups=mesh['dp'=2,'row'=4,'col'=4] {'dp','row','col'}, use_global_device_ids=true, to_apply=%region_41.42 | all-reduce | flops 8192 | bytes 65536 | tf_op jit(solution)/shard_map/psum | solution.py:186
  (344 shorter events, 438.7 us)
Async XLA Ops:
  8.7 105.5 %all-gather.15.cloned.1.call-start = ((), (), s32[]{:S(2)}) async-start(), calls=%async_computation.22 | async-start | bytes 2621440 | tf_op jit(solution)/shard_map/all_gather | solution.py:43
  24.0 132.5 %all-gather.19.cloned.1.call-start = ((), (), s32[]{:S(2)}) async-start(), calls=%async_computation.24 | async-start | bytes 2228224 | tf_op jit(solution)/shard_map/all_gather | solution.py:43
  71.9 131.5 %all-gather.21.cloned.1.call-start = ((), (), s32[]{:S(2)}) async-start(), calls=%async_computation.25 | async-start | bytes 2621440 | tf_op jit(solution)/shard_map/all_gather | solution.py:43
  81.8 197.1 %reduce-scatter.11.cloned.1.call-start = ((), (), s32[]{:S(2)}) async-start(), calls=%async_computation.26 | async-start | bytes 5242880 | tf_op jit(solution)/shard_map/reduce_scatter | solution.py:47
  209.8 136.9 %all-gather.27.cloned.1.call-start = ((), (), s32[]{:S(2)}) async-start(), calls=%async_computation.29 | async-start | bytes 5242880 | tf_op jit(solution)/shard_map/all_gather | solution.py:43
  228.5 173.5 %all-gather.29.cloned.1.call-start = ((), (), s32[]{:S(2)}) async-start(), calls=%async_computation.31 | async-start | bytes 9437184 | tf_op jit(solution)/shard_map/all_gather | solution.py:43
  258.7 225.6 %all-gather.25.cloned.1.call-start = ((), (), s32[]{:S(2)}) async-start(), calls=%async_computation.28 | async-start | bytes 5242880 | tf_op jit(solution)/shard_map/all_gather | solution.py:43
  278.8 260.5 %all-gather.23.cloned.1.call-start = ((), (), s32[]{:S(2)}) async-start(), calls=%async_computation.27 | async-start | bytes 9437184 | tf_op jit(solution)/shard_map/all_gather | solution.py:43
  284.7 361.2 %reduce-scatter.15.cloned.1.call-start = ((), (), s32[]{:S(2)}) async-start(), calls=%async_computation.32 | async-start | bytes 9437184 | tf_op jit(solution)/shard_map/reduce_scatter | solution.py:47
  574.5 146.1 %reduce-scatter.13.cloned.1.call-start = ((), (), s32[]{:S(2)}) async-start(), calls=%async_computation.30 | async-start | bytes 9437184 | tf_op jit(solution)/shard_map/reduce_scatter | solution.py:47
  589.9 170.5 %all-gather.31.cloned.1.call-start = ((), (), s32[]{:S(2)}) async-start(), calls=%async_computation.33 | async-start | bytes 5242880 | tf_op jit(solution)/shard_map/all_gather | solution.py:43
  725.8 184.9 %reduce-scatter.19.cloned.1.call-start = ((), (), s32[]{:S(2)}) async-start(), calls=%async_computation.35 | async-start | bytes 2228224 | tf_op jit(solution)/shard_map/reduce_scatter | solution.py:47
  849.0 140.3 %reduce-scatter.29.cloned.1.call-start = ((), (), s32[]{:S(2)}) async-start(), calls=%async_computation.42 | async-start | bytes 5242880 | tf_op jit(solution)/shard_map/reduce_scatter | solution.py:47
  865.0 203.8 %reduce-scatter.27.cloned.1.call-start = ((), (), s32[]{:S(2)}) async-start(), calls=%async_computation.40 | async-start | bytes 5242880 | tf_op jit(solution)/shard_map/reduce_scatter | solution.py:47
  879.6 235.8 %reduce-scatter.21.cloned.1.call-start = ((), (), s32[]{:S(2)}) async-start(), calls=%async_computation.36 | async-start | bytes 2621440 | tf_op jit(solution)/shard_map/reduce_scatter | solution.py:47
  898.1 262.6 %reduce-scatter.25.cloned.1.call-start = ((), (), s32[]{:S(2)}) async-start(), calls=%async_computation.39 | async-start | bytes 2621440 | tf_op jit(solution)/shard_map/reduce_scatter | solution.py:47
  904.3 283.8 %reduce-scatter.23.cloned.1.call-start = ((), (), s32[]{:S(2)}) async-start(), calls=%async_computation.37 | async-start | bytes 1310720 | tf_op jit(solution)/shard_map/reduce_scatter | solution.py:47
  913.4 309.3 %all-gather.35.cloned.1.call-start = ((), (), s32[]{:S(2)}) async-start(), calls=%async_computation.43 | async-start | bytes 3145728 | tf_op jit(solution)/shard_map/all_gather | solution.py:43
  1008.2 262.7 %reduce-scatter.17.cloned.1.call-start = ((), (), s32[]{:S(2)}) async-start(), calls=%async_computation.34 | async-start | bytes 5242880 | tf_op jit(solution)/shard_map/reduce_scatter | solution.py:47
  1014.2 291.6 %all-gather.33.cloned.1.call-start = ((), (), s32[]{:S(2)}) async-start(), calls=%async_computation.41 | async-start | bytes 3145728 | tf_op jit(solution)/shard_map/all_gather | solution.py:43
  1162.8 66.2 %all-to-all-start.8 = ((bf16[128,4,512]{2,0,1:T(8,128)(2,1)}), bf16[128,4,512]{2,0,1:T(8,128)(2,1)S(1)}, u32[]{:S(2)}, u32[]{:S(2)}) async-start(bf16[128,4,512]{2,0,1:T(8,128)(2,1)} %bitcast.353), calls=%async_computation.16 | async-start | bytes 1048576 | tf_op jit(solution)/shard_map/all_to_all | solution.py:39
  1166.2 213.6 %all-reduce.4.cloned.1.call-start = ((), (), s32[]{:S(2)}) async-start(), calls=%async_computation.38 | async-start | bytes 524288 | tf_op jit(solution)/shard_map/psum | solution.py:185
  1232.6 189.7 %all-reduce.6.cloned.1.call-start = ((), (), s32[]{:S(2)}) async-start(), calls=%async_computation.44 | async-start | bytes 2097152 | tf_op jit(solution)/shard_map/psum | solution.py:188
  1277.1 189.7 %all-to-all-start.6 = ((bf16[256,4,512]{2,0,1:T(8,128)(2,1)}), bf16[256,4,512]{2,0,1:T(8,128)(2,1)}, u32[]{:S(2)}, u32[]{:S(2)}) async-start(bf16[256,4,512]{2,0,1:T(8,128)(2,1)} %bitcast.351), calls=%async_computation.11 | async-start | bytes 2097152 | tf_op jit(solution)/shard_map/all_to_all | solution.py:39
  (65 other events, 1431.1 us)
Sparse Core Ops, SparseCore 0:
  9.6 37.4 all-gather.12
  48.7 17.0 all-gather.16
  67.9 46.2 all-gather.14
  116.8 39.6 all-gather.18
  158.4 44.9 all-gather.20
  209.9 53.9 reduce-scatter.10
  266.2 80.5 all-gather.26
  349.4 52.5 all-gather.28
  403.6 80.5 all-gather.24
  486.7 52.5 all-gather.22
  574.6 71.3 reduce-scatter.14
  649.2 71.2 reduce-scatter.12
  725.9 34.4 all-gather.30
  849.1 61.5 reduce-scatter.18
  913.4 75.7 reduce-scatter.28
  991.5 77.2 reduce-scatter.26
  1070.9 44.3 reduce-scatter.20
  1117.6 43.1 reduce-scatter.24
  1163.9 24.1 reduce-scatter.22
  1189.6 33.1 all-gather.34
  1226.0 44.8 reduce-scatter.16
  1273.0 32.7 all-gather.32
  1309.2 70.6 all-reduce.3
  1382.7 39.5 all-reduce.5
where the time goes:
time: 1480 us
  waiting for transfers between devices  955 us (65%)
  matrix products  214 us (14%)
  blocking collectives  155 us (10%)
  other arithmetic  73.4 us (5%)
  local copies, waits for them, and re-layouts  43.2 us (3%)
  starting transfers between devices  20.2 us (1%)
  between operations  16 us (1%)
    all_gather x12, waiting for transfers between devices, gather(): return lax.all_gather(x, axes, axis=dim, tiled=True)  445 us
    reduce_scatter x10, waiting for transfers between devices, scatter(): return lax.psum_scatter(x, axes, scatter_dimension=0, tiled=True)  391 us
    dot_general x63, matrix products, mm(): lax.dot_general(a, b, (((ca,), (cb,)), ((), ())), preferred_element_type=...  214 us
    all_to_all x4, blocking collectives, turn(): return lax.all_to_all(weight, 'col', 0, 1, tiled=True)  75.5 us
    psum x1, waiting for transfers between devices, local(): d_kv = lax.psum(d_kv, ('dp', 'row')).astype(F32)  69.8 us
    psum x1, waiting for transfers between devices, local(): d_query = lax.psum(turn_back(d_query), 'dp').astype(F32).T  40.7 us
    psum x1, blocking collectives, local(): lax.psum(jnp.stack([g_gain1, g_bias1, g_gain2, g_bias2]), ('dp', 'row', '...  39.5 us
    all_to_all x2, blocking collectives, turn_back(): return lax.all_to_all(rows, 'col', 1, 0, tiled=True)  34.6 us
  transfers between devices with their start and end apart: 29, of which 24 were waited for; matrix products, arithmetic and copies ran while one was open for 13% of the time, Pallas kernels for 0%

commit v1 on v0

--- a/solution.py
+++ b/solution.py
@@ -182,7 +182,7 @@
     back_one, g_gain1, g_bias1 = norm_backward(e_one, normed1, mine(inverse), gain1, keep_own)
     grad_in = turn_back((grad_middle + back_one).astype(BF))
     d_kv = scatter(mm(one_own, dkv_own, 0, 0).astype(BF), "col")
-    d_kv = lax.psum(d_kv, ("dp", "row")).astype(F32)
+    d_kv = jnp.sum(lax.all_gather(d_kv, ("dp", "row")), axis=0).astype(F32)
     small = lax.psum(jnp.stack([g_gain1, g_bias1, g_gain2, g_bias2]), ("dp", "row", "col"))
     small = lax.dynamic_slice_in_dim(small, col * f, f, 1)
     d_query = lax.psum(turn_back(d_query), "dp").astype(F32).T

time: 1480 us -> 1420 us (0.959)
  waiting for transfers between devices: 955 us -> 889 us
    psum x1 -> x0, waiting for transfers between devices: 69.8 us -> none  [local(): d_kv = lax.psum(d_kv, ('dp', 'row')).astype(F32)]
  transfers between devices with their start and end apart: 29 -> 29, of which waited for: 24 -> 25; matrix products, arithmetic and copies ran while one was open for 13% -> 14% of each run, Pallas kernels for 0% -> 0%
where the time goes in v1:
time: 1420 us; the launch traced here: 1410 us
  waiting for transfers between devices  889 us (63%)
  matrix products  214 us (15%)
  blocking collectives  156 us (11%)
  other arithmetic  74.4 us (5%)
  local copies, waits for them, and re-layouts  43.9 us (3%)
  starting transfers between devices  20.2 us (1%)
  between operations  16 us (1%)
    all_gather x12, waiting for transfers between devices, gather(): return lax.all_gather(x, axes, axis=dim, tiled=True)  445 us
    reduce_scatter x10, waiting for transfers between devices, scatter(): return lax.psum_scatter(x, axes, scatter_dimension=0, tiled=True)  383 us
    dot_general x63, matrix products, mm(): lax.dot_general(a, b, (((ca,), (cb,)), ((), ())), preferred_element_type=...  214 us
    all_to_all x4, blocking collectives, turn(): return lax.all_to_all(weight, 'col', 0, 1, tiled=True)  75.5 us
    psum x1, blocking collectives, local(): lax.psum(jnp.stack([g_gain1, g_bias1, g_gain2, g_bias2]), ('dp', 'row', '...  40.6 us
    psum x1, waiting for transfers between devices, local(): d_query = lax.psum(turn_back(d_query), 'dp').astype(F32).T  39.1 us
    all_to_all x2, blocking collectives, turn_back(): return lax.all_to_all(rows, 'col', 1, 0, tiled=True)  34.6 us
  transfers between devices with their start and end apart: 29, of which 25 were waited for; matrix products, arithmetic and copies ran while one was open for 14% of the time, Pallas kernels for 0%

profile of v1, /device:TPU:0, one launch (start us, length us, event | category | flops | bytes accessed | tf_op | source)
XLA Modules:
  0.0 1414.2 jit_solution(1557981959748297425)
XLA Ops:
  29.6 17.6 %all-gather.15.cloned.1.call-done = bf16[1024,2048]{1,0:T(8,128)(2,1)} async-done(((bf16[1024,512]{1,0:T(8,128)(2,1)}), bf16[1024,2048]{1,0:T(8,128)(2,1)}) %all-gather.15.cloned.1.call-update) | async-done | bytes 4194320 | tf_op jit(solution)/shard_map/all_gather | solution.py:43
  82.3 31.9 %all-gather.17.cloned.1.call-done = bf16[512,2048]{0,1:T(8,128)(2,1)} async-done(((bf16[128,2048]{0,1:T(8,128)(2,1)}), bf16[512,2048]{0,1:T(8,128)(2,1)}) %all-gather.17.cloned.1.call-update) | async-done | bytes 2097168 | tf_op jit(solution)/shard_map/all_gather | solution.py:43
  119.4 37.1 %all-gather.21.cloned.1.call-done = bf16[4096,256]{1,0:T(8,128)(2,1)} async-done(((bf16[256,256]{1,0:T(8,128)(2,1)}), bf16[4096,256]{1,0:T(8,128)(2,1)}) %all-gather.21.cloned.1.call-update) | async-done | bytes 2097168 | tf_op jit(solution)/shard_map/all_gather | solution.py:43
  184.7 18.8 %all-gather.23.cloned.1.call-done = bf16[512,2048]{0,1:T(8,128)(2,1)} async-done(((bf16[128,2048]{0,1:T(8,128)(2,1)}), bf16[512,2048]{0,1:T(8,128)(2,1)}) %all-gather.23.cloned.1.call-update) | async-done | bytes 2097168 | tf_op jit(solution)/shard_map/all_gather | solution.py:43
  210.0 17.2 %all_to_all.201 = bf16[4,256,512]{2,1,0:T(8,128)(2,1)S(1)} all-to-all(bf16[4,256,512]{2,1,0:T(8,128)(2,1)S(1)} %bitcast.407), channel_id=1, replica_groups=mesh['dp'=2,'row'=4,'col'=4] {'col'}, dimensions={0} | all-to-all | bytes 2097152 | tf_op jit(solution)/shard_map/all_to_all | solution.py:35
  229.1 28.4 %all_to_all.202 = bf16[4,256,512]{2,1,0:T(8,128)(2,1)S(1)} all-to-all(bf16[4,256,512]{2,1,0:T(8,128)(2,1)S(1)} %fusion.58), channel_id=1, replica_groups=mesh['dp'=2,'row'=4,'col'=4] {'col'}, dimensions={0} | all-to-all | bytes 2097152 | tf_op jit(solution)/shard_map/all_to_all | solution.py:35
  284.8 62.0 %all-gather.29.cloned.1.call-done = bf16[1024,2048]{0,1:T(8,128)(2,1)} async-done(((bf16[256,2048]{0,1:T(8,128)(2,1)}), bf16[1024,2048]{0,1:T(8,128)(2,1)}) %all-gather.29.cloned.1.call-update) | async-done | bytes 4194320 | tf_op jit(solution)/shard_map/all_gather | solution.py:43
  346.8 55.2 %all-gather.31.cloned.1.call-done = bf16[2048,2048]{1,0:T(8,128)(2,1)} async-done(((bf16[256,2048]{1,0:T(8,128)(2,1)}), bf16[2048,2048]{1,0:T(8,128)(2,1)}) %all-gather.31.cloned.1.call-update) | async-done | bytes 8388624 | tf_op jit(solution)/shard_map/all_gather | solution.py:43
  416.4 67.8 %all-gather.27.cloned.1.call-done = bf16[1024,2048]{0,1:T(8,128)(2,1)} async-done(((bf16[256,2048]{0,1:T(8,128)(2,1)}), bf16[1024,2048]{0,1:T(8,128)(2,1)}) %all-gather.27.cloned.1.call-update) | async-done | bytes 4194320 | tf_op jit(solution)/shard_map/all_gather | solution.py:43
  484.2 55.1 %all-gather.25.cloned.1.call-done = bf16[2048,2048]{1,0:T(8,128)(2,1)} async-done(((bf16[256,2048]{1,0:T(8,128)(2,1)}), bf16[2048,2048]{1,0:T(8,128)(2,1)}) %all-gather.25.cloned.1.call-update) | async-done | bytes 8388624 | tf_op jit(solution)/shard_map/all_gather | solution.py:43
  539.3 22.2 %fusion.6 = (bf16[2048,1024]{1,0:T(8,128)(2,1)S(1)}, f32[2048,1024]{1,0:T(8,128)}) fusion(f32[2048,1024]{1,0:T(8,128)} %fusion.125, bf16[2048,2048]{1,0:T(8,128)(2,1)} %all-gather.25.cloned.1.call-done, bf16[1024,2048]{0,1:T(8,128)(2,1)} %all-gather.27.cloned.1.call-done), kind=kOutput, calls=%fused_computation.11 | convolution fusion | flops 8631877632 | bytes 33554432 | tf_op jit(solution)/shard_map/dot_general | solution.py:12
  590.0 55.9 %reduce-scatter.15.cloned.1.call-done = bf16[256,2048]{1,0:T(8,128)(2,1)} async-done(((bf16[2048,2048]{1,0:T(8,128)(2,1)}), bf16[256,2048]{1,0:T(8,128)(2,1)}) %reduce-scatter.15.cloned.1.call-update) | async-done | bytes 1048592 | tf_op jit(solution)/shard_map/reduce_scatter | solution.py:47
  648.7 71.8 %reduce-scatter.13.cloned.1.call-done = bf16[256,2048]{1,0:T(8,128)(2,1)} async-done(((bf16[2048,2048]{1,0:T(8,128)(2,1)}), bf16[256,2048]{1,0:T(8,128)(2,1)}) %reduce-scatter.13.cloned.1.call-update) | async-done | bytes 1048592 | tf_op jit(solution)/shard_map/reduce_scatter | solution.py:47
  725.9 34.5 %all-gather.33.cloned.1.call-done = bf16[1024,2048]{1,0:T(8,128)(2,1)} async-done(((bf16[256,2048]{1,0:T(8,128)(2,1)}), bf16[1024,2048]{1,0:T(8,128)(2,1)}) %all-gather.33.cloned.1.call-update) | async-done | bytes 4194320 | tf_op jit(solution)/shard_map/all_gather | solution.py:43
  913.4 75.8 %reduce-scatter.29.cloned.1.call-done = bf16[256,2048]{1,0:T(8,128)(2,1)} async-done(((bf16[1024,2048]{1,0:T(8,128)(2,1)}), bf16[256,2048]{1,0:T(8,128)(2,1)}) %reduce-scatter.29.cloned.1.call-update) | async-done | bytes 1048592 | tf_op jit(solution)/shard_map/reduce_scatter | solution.py:47
  990.5 17.6 %all_to_all.204 = bf16[256,4,512]{2,0,1:T(8,128)(2,1)} all-to-all(bf16[256,4,512]{2,0,1:T(8,128)(2,1)S(1)} %bitcast.416), channel_id=1, replica_groups=mesh['dp'=2,'row'=4,'col'=4] {'col'}, dimensions={1} | all-to-all | bytes 2097152 | tf_op jit(solution)/shard_map/all_to_all | solution.py:39
  1014.3 54.5 %reduce-scatter.27.cloned.1.call-done = bf16[256,2048]{1,0:T(8,128)(2,1)} async-done(((bf16[1024,2048]{1,0:T(8,128)(2,1)}), bf16[256,2048]{1,0:T(8,128)(2,1)}) %reduce-scatter.27.cloned.1.call-update) | async-done | bytes 1048592 | tf_op jit(solution)/shard_map/reduce_scatter | solution.py:47
  1088.5 26.9 %reduce-scatter.21.cloned.1.call-done = bf16[128,2048]{1,0:T(8,128)(2,1)} async-done(((bf16[512,2048]{1,0:T(8,128)(2,1)}), bf16[128,2048]{1,0:T(8,128)(2,1)}) %reduce-scatter.21.cloned.1.call-update) | async-done | bytes 524304 | tf_op jit(solution)/shard_map/reduce_scatter | solution.py:47
  1120.7 40.1 %reduce-scatter.25.cloned.1.call-done = bf16[128,2048]{1,0:T(8,128)(2,1)} async-done(((bf16[512,2048]{1,0:T(8,128)(2,1)}), bf16[128,2048]{1,0:T(8,128)(2,1)}) %reduce-scatter.25.cloned.1.call-update) | async-done | bytes 524304 | tf_op jit(solution)/shard_map/reduce_scatter | solution.py:47
  1189.6 33.1 %all-gather.37.cloned.1.call-done = bf16[2048,512]{1,0:T(8,128)(2,1)} async-done(((bf16[1024,512]{1,0:T(8,128)(2,1)}), bf16[2048,512]{1,0:T(8,128)(2,1)}) %all-gather.37.cloned.1.call-update) | async-done | bytes 2097168 | tf_op jit(solution)/shard_map/all_gather | solution.py:43
  1231.5 39.1 %reduce-scatter.17.cloned.1.call-done = bf16[256,2048]{1,0:T(8,128)(2,1)} async-done(((bf16[1024,2048]{1,0:T(8,128)(2,1)}), bf16[256,2048]{1,0:T(8,128)(2,1)}) %reduce-scatter.17.cloned.1.call-update) | async-done | bytes 1048592 | tf_op jit(solution)/shard_map/reduce_scatter | solution.py:47
  1281.1 24.8 %all-gather.35.cloned.1.call-done = bf16[2048,512]{0,1:T(8,128)(2,1)} async-done(((bf16[1024,512]{0,1:T(8,128)(2,1)}), bf16[2048,512]{0,1:T(8,128)(2,1)}) %all-gather.35.cloned.1.call-update) | async-done | bytes 2097168 | tf_op jit(solution)/shard_map/all_gather | solution.py:43
  1310.0 39.1 %all-reduce.3.cloned.1.call-done = (bf16[512,512]{1,0:T(8,128)(2,1)}, bf16[512,512]{1,0:T(8,128)(2,1)}) async-done(((bf16[512,512]{1,0:T(8,128)(2,1)}, bf16[512,512]{1,0:T(8,128)(2,1)}), (bf16[512,512]{1,0:T(8,128)(2,1)}, bf16[512,512]{1,0:T(8,128)(2,1)})) %all-reduce.3.cloned.1.call-update) | async-done | bytes 1048592 | tf_op jit(solution)/shard_map/psum | solution.py:188
  1353.6 40.6 %psum.21 = f32[4,2048]{1,0:T(4,128)S(1)} all-reduce(f32[4,2048]{1,0:T(4,128)S(1)} %pad_maximum_fusion.2), channel_id=1, replica_groups=mesh['dp'=2,'row'=4,'col'=4] {'dp','row','col'}, use_global_device_ids=true, to_apply=%region_41.42 | all-reduce | flops 8192 | bytes 65536 | tf_op jit(solution)/shard_map/psum | solution.py:186
  (345 shorter events, 431.1 us)
Async XLA Ops:
  8.0 57.8 %all-gather.19.cloned.1.call-start = ((), (), s32[]{:S(2)}) async-start(), calls=%async_computation.23 | async-start | bytes 1310720 | tf_op jit(solution)/shard_map/all_gather | solution.py:43
  8.7 105.5 %all-gather.17.cloned.1.call-start = ((), (), s32[]{:S(2)}) async-start(), calls=%async_computation.22 | async-start | bytes 2621440 | tf_op jit(solution)/shard_map/all_gather | solution.py:43
  24.0 132.5 %all-gather.21.cloned.1.call-start = ((), (), s32[]{:S(2)}) async-start(), calls=%async_computation.24 | async-start | bytes 2228224 | tf_op jit(solution)/shard_map/all_gather | solution.py:43
  71.9 131.5 %all-gather.23.cloned.1.call-start = ((), (), s32[]{:S(2)}) async-start(), calls=%async_computation.25 | async-start | bytes 2621440 | tf_op jit(solution)/shard_map/all_gather | solution.py:43
  81.8 197.1 %reduce-scatter.11.cloned.1.call-start = ((), (), s32[]{:S(2)}) async-start(), calls=%async_computation.26 | async-start | bytes 5242880 | tf_op jit(solution)/shard_map/reduce_scatter | solution.py:47
  209.8 136.9 %all-gather.29.cloned.1.call-start = ((), (), s32[]{:S(2)}) async-start(), calls=%async_computation.29 | async-start | bytes 5242880 | tf_op jit(solution)/shard_map/all_gather | solution.py:43
  228.5 173.5 %all-gather.31.cloned.1.call-start = ((), (), s32[]{:S(2)}) async-start(), calls=%async_computation.31 | async-start | bytes 9437184 | tf_op jit(solution)/shard_map/all_gather | solution.py:43
  258.7 225.6 %all-gather.27.cloned.1.call-start = ((), (), s32[]{:S(2)}) async-start(), calls=%async_computation.28 | async-start | bytes 5242880 | tf_op jit(solution)/shard_map/all_gather | solution.py:43
  278.8 260.5 %all-gather.25.cloned.1.call-start = ((), (), s32[]{:S(2)}) async-start(), calls=%async_computation.27 | async-start | bytes 9437184 | tf_op jit(solution)/shard_map/all_gather | solution.py:43
  284.7 361.2 %reduce-scatter.15.cloned.1.call-start = ((), (), s32[]{:S(2)}) async-start(), calls=%async_computation.32 | async-start | bytes 9437184 | tf_op jit(solution)/shard_map/reduce_scatter | solution.py:47
  574.5 146.1 %reduce-scatter.13.cloned.1.call-start = ((), (), s32[]{:S(2)}) async-start(), calls=%async_computation.30 | async-start | bytes 9437184 | tf_op jit(solution)/shard_map/reduce_scatter | solution.py:47
  589.9 170.5 %all-gather.33.cloned.1.call-start = ((), (), s32[]{:S(2)}) async-start(), calls=%async_computation.33 | async-start | bytes 5242880 | tf_op jit(solution)/shard_map/all_gather | solution.py:43
  725.8 184.9 %reduce-scatter.19.cloned.1.call-start = ((), (), s32[]{:S(2)}) async-start(), calls=%async_computation.35 | async-start | bytes 2228224 | tf_op jit(solution)/shard_map/reduce_scatter | solution.py:47
  849.0 140.3 %reduce-scatter.29.cloned.1.call-start = ((), (), s32[]{:S(2)}) async-start(), calls=%async_computation.41 | async-start | bytes 5242880 | tf_op jit(solution)/shard_map/reduce_scatter | solution.py:47
  865.0 203.8 %reduce-scatter.27.cloned.1.call-start = ((), (), s32[]{:S(2)}) async-start(), calls=%async_computation.39 | async-start | bytes 5242880 | tf_op jit(solution)/shard_map/reduce_scatter | solution.py:47
  879.6 235.8 %reduce-scatter.21.cloned.1.call-start = ((), (), s32[]{:S(2)}) async-start(), calls=%async_computation.36 | async-start | bytes 2621440 | tf_op jit(solution)/shard_map/reduce_scatter | solution.py:47
  898.1 262.7 %reduce-scatter.25.cloned.1.call-start = ((), (), s32[]{:S(2)}) async-start(), calls=%async_computation.38 | async-start | bytes 2621440 | tf_op jit(solution)/shard_map/reduce_scatter | solution.py:47
  904.3 283.8 %reduce-scatter.23.cloned.1.call-start = ((), (), s32[]{:S(2)}) async-start(), calls=%async_computation.37 | async-start | bytes 1310720 | tf_op jit(solution)/shard_map/reduce_scatter | solution.py:47
  913.4 309.3 %all-gather.37.cloned.1.call-start = ((), (), s32[]{:S(2)}) async-start(), calls=%async_computation.42 | async-start | bytes 3145728 | tf_op jit(solution)/shard_map/all_gather | solution.py:43
  1008.2 262.5 %reduce-scatter.17.cloned.1.call-start = ((), (), s32[]{:S(2)}) async-start(), calls=%async_computation.34 | async-start | bytes 5242880 | tf_op jit(solution)/shard_map/reduce_scatter | solution.py:47
  1014.2 291.7 %all-gather.35.cloned.1.call-start = ((), (), s32[]{:S(2)}) async-start(), calls=%async_computation.40 | async-start | bytes 3145728 | tf_op jit(solution)/shard_map/all_gather | solution.py:43
  1166.1 182.9 %all-reduce.3.cloned.1.call-start = ((), (), s32[]{:S(2)}) async-start(), calls=%async_computation.44 | async-start | bytes 2097152 | tf_op jit(solution)/shard_map/psum | solution.py:188
  1175.8 225.0 %all-gather.39.cloned.1.call-start = ((), (), s32[]{:S(2)}) async-start(), calls=%async_computation.43 | async-start | bytes 2359296 | tf_op jit(solution)/shard_map/all_gather | solution.py:185
  1276.8 126.8 %all-to-all-start.6 = ((bf16[256,4,512]{2,0,1:T(8,128)(2,1)}), bf16[256,4,512]{2,0,1:T(8,128)(2,1)}, u32[]{:S(2)}, u32[]{:S(2)}) async-start(bf16[256,4,512]{2,0,1:T(8,128)(2,1)} %bitcast.352), calls=%async_computation.11 | async-start | bytes 2097152 | tf_op jit(solution)/shard_map/all_to_all | solution.py:39
  (65 other events, 1344.2 us)
Sparse Core Ops, SparseCore 0:
  9.6 37.4 all-gather.14
  48.7 17.0 all-gather.18
  67.9 46.2 all-gather.16
  116.8 39.6 all-gather.20
  158.4 44.9 all-gather.22
  209.9 53.9 reduce-scatter.10
  266.2 80.5 all-gather.28
  349.4 52.5 all-gather.30
  403.6 80.5 all-gather.26
  486.7 52.5 all-gather.24
  574.6 71.3 reduce-scatter.14
  649.2 71.2 reduce-scatter.12
  725.9 34.4 all-gather.32
  849.1 61.5 reduce-scatter.18
  913.4 75.7 reduce-scatter.28
  991.5 77.2 reduce-scatter.26
  1070.9 44.3 reduce-scatter.20
  1117.6 43.1 reduce-scatter.24
  1163.9 24.1 reduce-scatter.22
  1189.6 33.1 all-gather.36
  1226.0 44.5 reduce-scatter.16
  1272.7 33.0 all-gather.34
  1308.8 40.2 all-reduce.2
  1351.3 49.5 all-gather.38
